TPU v7x, 32 devices: a whole 2x2x4 slice. The times are simulated.
32 devices in a mesh: groups: 2 (over y), rows: 8 (over z, x), sub: 2 (over core).
Axes of the slice: x: 2, y: 2, z: 4, core: 2. Of those that a mesh axis runs over, the one named last changes fastest.
Arguments:
- coupling: bfloat16 [131072, 128], P(('groups', 'rows', 'sub')), parts along dimension 0, may hold values from 0.009 to 110
- tile_vals: bfloat16 [1024, 6, 128, 128], P(('groups', 'rows', 'sub')), parts along dimension 0, may hold values from -0.02734375 to 0.02734375
- tile_cols: int32 [1024, 6], P(('groups', 'rows', 'sub')), parts along dimension 0, may hold values from 0 to 511, as said below
- cluster_graph: int32 [256, 128], P('groups'), parts along dimension 0, may hold values from 0 to 3
- cluster_mass: float32 [256], P('groups'), parts along dimension 0, may hold values from 0.25 to 4
Outputs:
- log_coupling: float32 [131072, 128], P(('groups', 'rows', 'sub')), parts along dimension 0
There are 2 independent parts, one for each index of `groups`. A program takes and returns all parts, laid end to end along the dimension named above; each array names one. Nothing has to cross between parts.
Inputs may be any that keep to these rules, and one draw needn't show every extreme that they name: `tile_cols`: within each device's rows of 32 block rows, a slot below 4 names a column block held by the same device or by the device just before or after it along rows+sub. Over the slots from 4 on, the block rows of one device name column blocks held by any one device at most 4 times, and some device exactly 4 times.
All inputs are finite; a program needn't handle non-finite values.
Results may differ from a plain program's by a relative error of at most 0.0003.
Values may be sent and summed in bfloat16 or wider, within the bound.
No kernel may reach another device: no remote copies, remote signals or barrier semaphores. Data moves between devices by JAX's collectives and lax.ppermute only.
A program may use at most 128 MiB of HBM per device.

v0:
```python
import jax
import jax.numpy as jnp
from jax import lax
from jax.sharding import PartitionSpec as P

NEAR = 4


eta_step = 2.0
relax_power = 0.5


def padded(cells, sides, width):
    for axis, dim in sides:
        count = lax.axis_size(axis)
        ends = count - 1
        head = lax.slice_in_dim(cells, 0, width, axis=dim)
        tail = lax.slice_in_dim(cells, cells.shape[dim] - width, cells.shape[dim], axis=dim)
        cells = jnp.concatenate(
            [
                lax.ppermute(tail, axis, [(i, (i + 1) % count) for i in range(ends)]),
                cells,
                lax.ppermute(head, axis, [((i + 1) % count, i) for i in range(ends)]),
            ],
            axis=dim,
        )
    return cells


def local(coupling, tile_vals, tile_cols, cluster_graph, cluster_mass):
    shards = lax.axis_size(("rows", "sub"))
    my_index = lax.axis_index(("rows", "sub"))
    blocks_dev = tile_cols.shape[0]
    tile_size = tile_vals.shape[2]
    clusters = coupling.shape[1]
    far_slots = tile_cols.shape[1] - NEAR
    nodes_total = blocks_dev * tile_size * shards
    blocks_local = coupling.reshape(blocks_dev, tile_size, clusters)
    window = padded(coupling, ((("rows", "sub"), 0),), blocks_dev * tile_size)
    window = window.reshape(3 * blocks_dev, tile_size, clusters)
    near_index = tile_cols[:, :NEAR] - (my_index * blocks_dev - blocks_dev)
    spread = jnp.zeros((blocks_dev, tile_size, clusters), jnp.float32)
    for slot_id in range(NEAR):
        picked = jnp.take(window, near_index[:, slot_id], axis=0)
        spread = spread + jnp.einsum(
            "nij,njk->nik", tile_vals[:, slot_id], picked, preferred_element_type=jnp.float32
        )
    far_count = blocks_dev * far_slots
    capacity = (far_count + shards - 1) // shards
    far_cols = tile_cols[:, NEAR:].reshape(far_count)
    far_owner = far_cols // blocks_dev
    far_local = far_cols % blocks_dev
    owner_hits = (far_owner[:, None] == jnp.arange(shards, dtype=jnp.int32)[None, :]).astype(
        jnp.int32
    )
    earlier = jnp.cumsum(owner_hits, axis=0) - owner_hits
    far_slot = jnp.sum(earlier * owner_hits, axis=1)
    requests = jnp.zeros((shards, capacity), jnp.int32).at[far_owner, far_slot].set(far_local)
    found = jnp.take(
        blocks_local,
        lax.all_to_all(requests, ("rows", "sub"), split_axis=0, concat_axis=0, tiled=True),
        axis=0,
    )
    fetched = lax.all_to_all(found, ("rows", "sub"), split_axis=0, concat_axis=0, tiled=True)
    far_blocks = fetched[far_owner, far_slot]
    far_tiles = tile_vals[:, NEAR:].reshape(far_count, tile_size, tile_size)
    far_terms = jnp.einsum(
        "nij,njk->nik", far_tiles, far_blocks, preferred_element_type=jnp.float32
    )
    spread = spread + jnp.sum(far_terms.reshape(blocks_dev, far_slots, tile_size, clusters), axis=1)
    spread = spread.reshape(blocks_dev * tile_size, clusters)
    graph = cluster_graph.astype(jnp.float32)
    affinity = jnp.dot(spread, graph.T / clusters, precision=lax.Precision.HIGHEST)
    whole = coupling.astype(jnp.float32)
    mass_part = jnp.sum(whole, axis=0) / nodes_total
    boosted = jnp.log(whole) + 2.0 * eta_step * affinity
    boost_part = jnp.sum(jnp.exp(boosted), axis=0) / nodes_total
    colmass, boost_mass = lax.psum((mass_part, boost_part), ("rows", "sub"))
    pull = jnp.dot(graph * graph, colmass, precision=lax.Precision.HIGHEST) / clusters
    logits = boosted - eta_step * pull[None, :]
    log_new = jnp.log(boost_mass) - eta_step * pull
    shifted = logits + relax_power * (jnp.log(cluster_mass) - log_new)[None, :]
    return shifted - jnp.log(jnp.sum(jnp.exp(shifted), axis=1, keepdims=True))


def solution(mesh):
    return jax.shard_map(
        local,
        mesh=mesh,
        in_specs=(
            P(("groups", "rows", "sub"), None),
            P(("groups", "rows", "sub"), None, None, None),
            P(("groups", "rows", "sub"), None),
            P("groups", None),
            P("groups"),
        ),
        out_specs=P(("groups", "rows", "sub"), None),
        check_vma=False,
    )
```

profile of v0, /device:TPU:16, one launch (start us, length us, event | category | flops | bytes accessed | tf_op | source)
XLA Modules:
  0.0 167.3 jit_solution(341923318796550742)
XLA Ops:
  0.0 0.8 slice.42
  0.8 0.1 copy.27
  0.9 0.1 reshape.172
  1.0 0.1 reshape.171
  1.1 0.1 fusion.31
  1.2 0.1 reduce_window_sum.11
  1.3 0.2 select_reduce_fusion
  1.5 3.5 %scatter_fusion = s32[16,4]{0,1:T(4,128)S(1)} fusion(s32[16,4]{0,1:T(4,128)S(1)} %broadcast_in_dim.33, s32[64]{0:T(128)S(1)} %fusion.34, s32[64]{0:T(128)S(1)} %get-tuple-element.24), kind=kCustom, calls=%fused_computation.6 | custom fusion | bytes 1280 | tf_op jit(solution)/shard_map/scatter | solution.py:58
  5.0 0.1 copy.29
  5.1 10.1 %all_to_all.20 = s32[16,1,4]{2,1,0:T(1,128)S(1)} all-to-all(s32[16,1,4]{2,1,0:T(1,128)S(1)} %copy.29), channel_id=1, replica_groups=mesh['groups'=2,'rows'=8,'sub'=2] {'rows','sub'}, dimensions={0} | all-to-all | bytes 512 | tf_op jit(solution)/shard_map/all_to_all | solution.py:61
  15.2 0.1 copy.30
  15.3 0.1 copy.33
  15.3 0.1 reshape.211
  15.4 0.1 copy.31
  15.5 0.0 copy-done
  15.5 0.9 gather_fusion
  16.5 1.6 broadcast_select_fusion
  18.1 6.7 %all-to-all-start.1 = ((bf16[16,4,128,128]{3,2,1,0:T(8,128)(2,1)}), bf16[16,4,128,128]{3,2,1,0:T(8,128)(2,1)}, u32[]{:S(2)}, u32[]{:S(2)}) async-start(bf16[16,4,128,128]{3,2,1,0:T(8,128)(2,1)} %broadcast_select_fusion), calls=%async_computation.1 | async-start | bytes 4194304 | tf_op jit(solution)/shard_map/all_to_all | solution.py:64
  24.8 2.0 %collective-permute-start = (bf16[4096,128]{1,0:T(8,128)(2,1)S(1)}, bf16[4096,128]{1,0:T(8,128)(2,1)S(1)}, u32[]{:S(2)}, u32[]{:S(2)}) collective-permute-start(bf16[4096,128]{1,0:T(8,128)(2,1)S(1)} %copy-done), channel_id=1, source_target_pairs={{0,1},{1,2},{2,3},{3,4},{4,5},{5,6},{6,7},{7,8},{8,9},{9,10},{10,1... | collective-permute-start | bytes 3145736 | tf_op jit(solution)/shard_map/ppermute | solution.py:21
  26.9 4.4 %collective-permute-start.1 = (bf16[4096,128]{1,0:T(8,128)(2,1)S(1)}, bf16[4096,128]{1,0:T(8,128)(2,1)S(1)}, u32[]{:S(2)}, u32[]{:S(2)}) collective-permute-start(bf16[4096,128]{1,0:T(8,128)(2,1)S(1)} %copy-done), channel_id=1, source_target_pairs={{1,0},{2,1},{3,2},{4,3},{5,4},{6,5},{7,6},{8,7},{9,8},{10,9},{11,1... | collective-permute-start | bytes 3145736 | tf_op jit(solution)/shard_map/ppermute | solution.py:23
  31.3 0.0 copy-done.4
  31.4 0.6 convert_reduce_fusion
  32.0 51.8 %collective-permute-done = bf16[4096,128]{1,0:T(8,128)(2,1)S(1)} collective-permute-done((bf16[4096,128]{1,0:T(8,128)(2,1)S(1)}, bf16[4096,128]{1,0:T(8,128)(2,1)S(1)}, u32[]{:S(2)}, u32[]{:S(2)}) %collective-permute-start) | collective-permute-done | bytes 1048608 | tf_op jit(solution)/shard_map/ppermute | solution.py:21
  83.8 0.0 collective-permute-done.1
  83.8 16.4 %pad_maximum_fusion = bf16[12288,128]{1,0:T(8,128)(2,1)} fusion(bf16[4096,128]{1,0:T(8,128)(2,1)S(1)} %collective-permute-done.1, bf16[4096,128]{1,0:T(8,128)(2,1)S(1)} %copy-done, bf16[4096,128]{1,0:T(8,128)(2,1)S(1)} %collective-permute-done), kind=kLoop, calls=%fused_computation.10 | loop fusion | flops 9437184 | bytes 6291456 | tf_op jit(solution)/shard_map/concatenate | solution.py:19
  100.2 3.6 %gather_fusion.4 = bf16[32,128,128]{2,1,0:T(8,128)(2,1)} fusion(bf16[96,128,128]{2,1,0:T(8,128)(2,1)} %bitcast.80, s32[1024]{0:T(1024)S(1)} %get-tuple-element.30), kind=kCustom, calls=%fused_computation.2.clone | custom fusion | bytes 2097280 | tf_op jit(solution)/shard_map/jit(_take)/gather | solution.py:44
  103.8 3.6 %gather_fusion.3 = bf16[32,128,128]{2,1,0:T(8,128)(2,1)} fusion(bf16[96,128,128]{2,1,0:T(8,128)(2,1)} %bitcast.81, s32[1024]{0:T(1024)S(1)} %get-tuple-element.31), kind=kCustom, calls=%fused_computation.1.clone | custom fusion | bytes 2097280 | tf_op jit(solution)/shard_map/jit(_take)/gather | solution.py:44
  107.4 3.7 %gather_fusion.2 = bf16[32,128,128]{2,1,0:T(8,128)(2,1)} fusion(bf16[96,128,128]{2,1,0:T(8,128)(2,1)} %bitcast.82, s32[1024]{0:T(1024)S(1)} %pad_clamp_fusion.4), kind=kCustom, calls=%fused_computation.clone | custom fusion | bytes 2097280 | tf_op jit(solution)/shard_map/jit(_take)/gather | solution.py:44
  111.1 3.5 %gather_fusion.5 = bf16[32,128,128]{2,1,0:T(8,128)(2,1)} fusion(bf16[96,128,128]{2,1,0:T(8,128)(2,1)} %bitcast.83, s32[1024]{0:T(1024)S(1)} %pad_clamp_fusion.1), kind=kCustom, calls=%fused_computation.3.clone | custom fusion | bytes 2097280 | tf_op jit(solution)/shard_map/jit(_take)/gather | solution.py:44
  114.6 3.5 %fusion.4 = f32[32,128,128]{1,2,0:T(8,128)} fusion(bf16[32,128,128]{2,1,0:T(8,128)(2,1)} %gather_fusion.4, bf16[32,6,128,128]{3,2,1,0:T(8,128)(2,1)} %param.8, pred[32]{0:T(512)(128)(4,1)S(1)} %get-tuple-element.18), kind=kOutput, calls=%fused_computation.22 | convolution fusion | flops 134742016 | bytes 4194336 | tf_op jit(solution)/shard_map/nij,njk->nik/dot_general | solution.py:45
  118.2 3.5 %fusion.6 = f32[32,128,128]{1,2,0:T(8,128)} fusion(bf16[32,128,128]{2,1,0:T(8,128)(2,1)} %gather_fusion.3, bf16[32,6,128,128]{3,2,1,0:T(8,128)(2,1)} %param.8, pred[32]{0:T(512)(128)(4,1)S(1)} %get-tuple-element.20), kind=kOutput, calls=%fused_computation.24 | convolution fusion | flops 134742016 | bytes 4194336 | tf_op jit(solution)/shard_map/nij,njk->nik/dot_general | solution.py:45
  121.7 0.0 slice-done
  121.7 0.0 slice-done.1
  121.7 0.0 copy-done.2
  121.7 1.9 %fusion.8 = f32[32,128,128]{1,2,0:T(8,128)} fusion(bf16[32,128,128]{2,1,0:T(8,128)(2,1)S(1)} %copy-done.2, bf16[32,6,128,128]{3,2,1,0:T(8,128)(2,1)S(1)} %bitcast.85, pred[32]{0:T(512)(128)(4,1)S(1)} %get-tuple-element.22), kind=kOutput, calls=%fused_computation.26 | convolution fusion | flops 134742016 | bytes 4194816 | tf_op jit(solution)/shard_map/nij,njk->nik/dot_general | solution.py:45
  123.6 0.0 all-to-all-done.1
  123.6 3.9 %gather_fusion.1 = bf16[64,128,128]{2,1,0:T(8,128)(2,1)} fusion(bf16[16,4,128,128]{3,2,1,0:T(8,128)(2,1)} %all-to-all-done.1, s32[64]{0:T(128)S(1)} %get-tuple-element.16), kind=kCustom, calls=%fused_computation.5 | custom fusion | bytes 4194816 | tf_op jit(solution)/shard_map/gather | solution.py:65
  127.5 0.0 slice-done.2
  127.5 4.6 %bitcast_reduce_fusion = f32[32,128,128]{1,2,0:T(8,128)} fusion(bf16[64,128,128]{2,1,0:T(8,128)(2,1)} %gather_fusion.1, bf16[64,128,128]{2,1,0:T(8,128)(2,1)S(1)} %bitcast.86), kind=kOutput, calls=%fused_computation.9 | convolution fusion | flops 268959744 | bytes 6291456 | tf_op jit(solution)/shard_map/nij,njk->nik/dot_general | solution.py:67
  132.2 3.0 %copy.35 = f32[32,128,128]{2,1,0:T(8,128)} copy(f32[32,128,128]{1,2,0:T(8,128)} %bitcast_reduce_fusion) | data formatting | bytes 4194304 | tf_op jit(solution)/shard_map/reduce_sum | solution.py:70
  135.2 0.0 copy-done.1
  135.2 4.2 %bitcast_add_fusion = f32[32,128,128]{2,1,0:T(8,128)S(1)} fusion(f32[32,128,128]{2,1,0:T(8,128)} %copy.35, f32[32,128,128]{1,2,0:T(8,128)S(1)} %copy-done.1, f32[32,128,128]{1,2,0:T(8,128)} %fusion.8, f32[32,128,128]{1,2,0:T(8,128)} %fusion.6, bf16[32,128,128]{2,1,0:T(8,128)(2,1)} %gather_fusion.5, bf16[32,6,128,128]{3,2,1,0:T(8,128)(2,1)} %param.8, ...), kind=kOutput, calls=%fused_computation.13 | convolution fusion | flops 136839168 | bytes 12582944 | tf_op jit(solution)/shard_map/nij,njk->nik/dot_general | solution.py:45
  139.4 0.0 copy-start.5
  139.4 2.1 %exponential_reduce_fusion.1 = (f32[128]{0:T(128)S(1)}, f32[4096,128]{1,0:T(8,128)S(1)}) fusion(f32[4096,128]{1,0:T(8,128)S(1)} %bitcast.87, s32[128,128]{1,0:T(8,128)S(1)} %copy-done.3, bf16[4096,128]{1,0:T(8,128)(2,1)S(1)} %copy-done), kind=kOutput, calls=%fused_computation.15 | convolution fusion | flops 807436160 | bytes 5308928 | tf_op jit(solution)/shard_map/dot_general | solution.py:73
  141.5 23.2 %all-reduce = (f32[128]{0:T(128)S(1)}, f32[128]{0:T(128)S(1)}) all-reduce(f32[128]{0:T(128)S(1)} %broadcast_multiply_fusion.1, f32[128]{0:T(128)S(1)} %broadcast_multiply_fusion), channel_id=1, replica_groups=mesh['groups'=2,'rows'=8,'sub'=2] {'rows','sub'}, use_global_device_ids=true, to_apply=%region_5.7 | all-reduce | flops 256 | bytes 2048 | tf_op jit(solution)/shard_map/psum | solution.py:78
  164.7 0.2 subtract_multiply_fusion
  164.9 0.7 exponential_reduce_fusion
  165.6 1.7 %fusion.1 = f32[4096,128]{1,0:T(8,128)} fusion(f32[4096,128]{1,0:T(8,128)S(1)} %get-tuple-element.27, f32[4096]{0:T(1024)S(1)} %log.20, f32[128]{0:T(128)S(1)} %get-tuple-element.28, f32[128]{0:T(128)S(1)} %get-tuple-element.29), kind=kLoop, calls=%fused_computation.18 | loop fusion | flops 1572864 | bytes 4211712 | tf_op jit(solution)/shard_map/sub | solution.py:83
  (26 shorter events, 0.1 us)
Async XLA Ops:
  0.0 15.5 %copy-start = (bf16[4096,128]{1,0:T(8,128)(2,1)S(1)}, bf16[4096,128]{1,0:T(8,128)(2,1)}, u32[]{:S(2)}) copy-start(bf16[4096,128]{1,0:T(8,128)(2,1)} %param.7) | copy-start | bytes 3145732
  18.1 13.2 %copy-start.4 = (s32[32,6]{0,1:T(8,128)S(1)}, s32[32,6]{0,1:T(8,128)}, u32[]{:S(2)}) copy-start(s32[32,6]{0,1:T(8,128)} %param.9) | copy-start | bytes 2308
  18.1 105.5 %all-to-all-start.1 = ((bf16[16,4,128,128]{3,2,1,0:T(8,128)(2,1)}), bf16[16,4,128,128]{3,2,1,0:T(8,128)(2,1)}, u32[]{:S(2)}, u32[]{:S(2)}) async-start(bf16[16,4,128,128]{3,2,1,0:T(8,128)(2,1)} %broadcast_select_fusion), calls=%async_computation.1 | async-start | bytes 4194304 | tf_op jit(solution)/shard_map/all_to_all | solution.py:64
  24.8 58.9 %collective-permute-start = (bf16[4096,128]{1,0:T(8,128)(2,1)S(1)}, bf16[4096,128]{1,0:T(8,128)(2,1)S(1)}, u32[]{:S(2)}, u32[]{:S(2)}) collective-permute-start(bf16[4096,128]{1,0:T(8,128)(2,1)S(1)} %copy-done), channel_id=1, source_target_pairs={{0,1},{1,2},{2,3},{3,4},{4,5},{5,6},{6,7},{7,8},{8,9},{9,10},{10,1... | collective-permute-start | bytes 3145736 | tf_op jit(solution)/shard_map/ppermute | solution.py:21
  26.9 56.9 %collective-permute-start.1 = (bf16[4096,128]{1,0:T(8,128)(2,1)S(1)}, bf16[4096,128]{1,0:T(8,128)(2,1)S(1)}, u32[]{:S(2)}, u32[]{:S(2)}) collective-permute-start(bf16[4096,128]{1,0:T(8,128)(2,1)S(1)} %copy-done), channel_id=1, source_target_pairs={{1,0},{2,1},{3,2},{4,3},{5,4},{6,5},{7,6},{8,7},{9,8},{10,9},{11,1... | collective-permute-start | bytes 3145736 | tf_op jit(solution)/shard_map/ppermute | solution.py:23
  107.4 14.3 %slice-start = ((s8[6291456]{0:T(1024)(128)(4,1)}), s8[2097152]{0:T(1024)(128)(4,1)S(1)}, s32[]{:S(2)}) async-start(s8[6291456]{0:T(1024)(128)(4,1)} %bitcast.84), calls=%async_computation.2 | async-start | bytes 4194304
  114.6 7.1 %slice-start.1 = ((s8[6291456]{0:T(1024)(128)(4,1)}), s8[4194304]{0:T(1024)(128)(4,1)S(1)}, s32[]{:S(2)}) async-start(s8[6291456]{0:T(1024)(128)(4,1)} %bitcast.84), calls=%async_computation.3 | async-start | bytes 8388608
  118.2 3.5 %copy-start.2 = (bf16[32,128,128]{2,1,0:T(8,128)(2,1)S(1)}, bf16[32,128,128]{2,1,0:T(8,128)(2,1)}, u32[]{:S(2)}) copy-start(bf16[32,128,128]{2,1,0:T(8,128)(2,1)} %gather_fusion.2) | copy-start | bytes 3145732
  123.6 3.9 %slice-start.2 = ((bf16[32,6,128,128]{3,2,1,0:T(8,128)(2,1)}), bf16[32,2,128,128]{3,2,1,0:T(8,128)(2,1)S(1)}, s32[]{:S(2)}) async-start(bf16[32,6,128,128]{3,2,1,0:T(8,128)(2,1)} %param.8), calls=%async_computation.4 | async-start | bytes 4194304 | tf_op jit(solution)/shard_map/slice | solution.py:66
  132.2 3.0 %copy-start.1 = (f32[32,128,128]{1,2,0:T(8,128)S(1)}, f32[32,128,128]{1,2,0:T(8,128)}, u32[]{:S(2)}) copy-start(f32[32,128,128]{1,2,0:T(8,128)} %fusion.4) | copy-start | bytes 6291460
  135.2 4.2 %copy-start.3 = (s32[128,128]{1,0:T(8,128)S(1)}, s32[128,128]{1,0:T(8,128)}, u32[]{:S(2)}) copy-start(s32[128,128]{1,0:T(8,128)} %param.10) | copy-start | bytes 196612
  139.4 25.3 %copy-start.5 = (f32[128]{0:T(128)S(1)}, f32[128]{0:T(128)}, u32[]{:S(2)}) copy-start(f32[128]{0:T(128)} %param.11) | copy-start | bytes 1540
where the time goes:
time: 168 us; the launch traced here: 167 us
  waiting for transfers between devices  51.8 us (31%)
  blocking collectives  33.3 us (20%)
  local copies, waits for them, and re-layouts  27.4 us (16%)
  other arithmetic  21.3 us (13%)
  matrix products  20.1 us (12%)
  starting transfers between devices  13.2 us (8%)
    ppermute x1, waiting for transfers between devices, padded(): lax.ppermute(tail, axis, [(i, (i + 1) % count) for i in range(ends)])  51.8 us
    psum x1, blocking collectives, local(): colmass, boost_mass = lax.psum((mass_part, boost_part), ('rows', 'sub'))  23.2 us
    concatenate x1, other arithmetic, padded(): jnp.concatenate([lax.ppermute(tail, axis, [(i, (i + 1) % count) for i in...  16.4 us
    gather x4, local copies, waits for them, and re-layouts, local(): picked = jnp.take(window, near_index[:, slot_id], axis=0)  14.5 us
    dot_general x4, matrix products, local(): jnp.einsum('nij,njk->nik', tile_vals[:, slot_id], picked, preferred_eleme...  13.1 us
    all_to_all x1, blocking collectives, local(): lax.all_to_all(requests, ('rows', 'sub'), split_axis=0, concat_axis=0, ti...  10.1 us
    all_to_all x1, starting transfers between devices, local(): lax.all_to_all(found, ('rows', 'sub'), split_axis=0, concat_axis=0, tiled...  6.75 us
    dot_general x1, matrix products, local(): jnp.einsum('nij,njk->nik', far_tiles, far_blocks, preferred_element_type=...  4.64 us
  transfers between devices with their start and end apart: 3, of which 1 were waited for; matrix products, arithmetic and copies ran while one was open for 24% of the time, Pallas kernels for 0%

commit v1 on v0

v1 whole, which is shorter than its diff:
```python
import functools

import jax
import jax.numpy as jnp
from jax import lax
from jax.experimental import pallas as pl
from jax.experimental.pallas import tpu as pltpu
from jax.sharding import PartitionSpec as P

NEAR = 4
NODES = ("rows", "sub")

eta_step = 2.0
relax_power = 0.5

ANY = pl.BlockSpec(memory_space=pl.ANY)
VMEM = pl.BlockSpec(memory_space=pltpu.VMEM)
SMEM = pl.BlockSpec(memory_space=pltpu.SMEM)


def requests_kernel(cap, nodes_total, cols_ref, coupling_ref, out_ref):
    blocks_dev, slots = cols_ref.shape
    shards = out_ref.shape[0]
    clusters = coupling_ref.shape[1]
    owner = lax.broadcasted_iota(jnp.int32, (blocks_dev, shards), 1)
    place = lax.broadcasted_iota(jnp.int32, (blocks_dev, clusters), 1).astype(jnp.float32)
    before = (
        lax.broadcasted_iota(jnp.int32, (blocks_dev, blocks_dev), 1)
        < lax.broadcasted_iota(jnp.int32, (blocks_dev, blocks_dev), 0)
    ).astype(jnp.float32)
    count = jnp.zeros((1, shards), jnp.float32)
    table = jnp.zeros((shards, clusters), jnp.float32)
    for slot_id in range(NEAR, slots):
        local = cols_ref[:, slot_id : slot_id + 1] - owner * blocks_dev
        hit = (local >= 0) & (local < blocks_dev)
        hits = hit.astype(jnp.float32)
        earlier = jnp.dot(before, hits, preferred_element_type=jnp.float32) + count
        rank = jnp.sum(earlier * hits, axis=1, keepdims=True)
        count = count + jnp.sum(hits, axis=0, keepdims=True)
        wanted = jnp.where(hit, local, 0).astype(jnp.float32)
        table = table + lax.dot_general(
            wanted,
            (rank == place).astype(jnp.float32),
            (((0,), (0,)), ((), ())),
            precision=lax.Precision.HIGHEST,
            preferred_element_type=jnp.float32,
        )
    rows = coupling_ref.shape[0]
    step = rows // 8

    def add(i, total):
        part = coupling_ref[pl.ds(pl.multiple_of(i * step, step), step), :].astype(jnp.float32)
        return total + jnp.sum(part.reshape(step // 8, 8, clusters), axis=0)

    total = lax.fori_loop(0, 8, add, jnp.zeros((8, clusters), jnp.float32))
    mass = jnp.sum(total, axis=0, keepdims=True) / nodes_total
    out_ref[:, :clusters] = jnp.broadcast_to(mass, (shards, clusters))
    out_ref[:, clusters:] = table


def gather_kernel(wanted_ref, blocks_ref, out_ref, sem):
    count = out_ref.shape[0]

    @pl.loop(0, count)
    def _(n):
        pltpu.make_async_copy(blocks_ref.at[wanted_ref[n]], out_ref.at[n], sem).start()

    pltpu.make_async_copy(out_ref, out_ref, sem).wait()


def split(x):
    high = x.astype(jnp.bfloat16)
    return jnp.concatenate([high, (x - high.astype(jnp.float32)).astype(jnp.bfloat16)], axis=1)


def near_kernel(
    group, cap, cols_ref, base_ref, left_ref, own_ref, right_ref, tiles_ref, rows_ref, graph_ref, mass_ref,
    part_ref, graph2_ref, where_ref, window, pull_ref, count_ref, sems,
):
    step = pl.program_id(0)
    blocks_dev, tile, clusters = own_ref.shape
    slots = cols_ref.shape[0] // blocks_dev

    @pl.when(step == 0)
    def _():
        copies = [
            pltpu.make_async_copy(src, window.at[pl.ds(i * blocks_dev, blocks_dev)], sems.at[i])
            for i, src in enumerate((left_ref, own_ref, right_ref))
        ]
        for copy in copies:
            copy.start()
        graph = graph_ref[...].astype(jnp.float32)
        colmass = jnp.sum(mass_ref[:, :clusters], axis=0, keepdims=True)
        pull_ref[...] = (
            lax.dot_general(
                jnp.broadcast_to(colmass, (8, clusters)),
                graph * graph,
                (((1,), (1,)), ((), ())),
                precision=lax.Precision.HIGHEST,
                preferred_element_type=jnp.float32,
            )
            / clusters
        )
        turned = graph.T.astype(jnp.bfloat16)
        graph2_ref[:clusters, :] = turned
        graph2_ref[clusters:, :] = turned

        shards = mass_ref.shape[0]

        @pl.loop(0, shards)
        def _(o):
            count_ref[o] = 0

        @pl.loop(0, blocks_dev)
        def _(b):
            pass

        for slot_id in range(NEAR, slots):

            @pl.loop(0, blocks_dev)
            def _(b):
                owner = cols_ref[b * slots + slot_id] // blocks_dev
                rank = count_ref[owner]
                count_ref[owner] = rank + 1
                where_ref[b * (slots - NEAR) + slot_id - NEAR] = owner * cap + rank

        for copy in copies:
            copy.wait()

    scale = 2.0 * eta_step / clusters
    for i in range(group):
        b = step * group + i
        picked = [window[cols_ref[b * slots + s] - base_ref[0]] for s in range(NEAR)]
        tiles = jnp.concatenate([tiles_ref[i, s] for s in range(NEAR)], axis=1)
        spread = jnp.dot(tiles, jnp.concatenate(picked, axis=0), preferred_element_type=jnp.float32)
        affinity = jnp.dot(split(spread), graph2_ref[...], preferred_element_type=jnp.float32)
        here = pl.ds(i * tile, tile)
        part_ref[here, :] = (
            jnp.log(rows_ref[here, :].astype(jnp.float32)) - eta_step * pull_ref[0:1, :] + scale * affinity
        )


def far_kernel(group, nodes_total, where_ref, blocks_ref, tiles_ref, part_ref, graph2_ref, logits_ref, mass_ref, total):
    step = pl.program_id(0)
    far_slots, tile, clusters = tiles_ref.shape[1:]

    @pl.when(step == 0)
    def _():
        total[...] = jnp.zeros_like(total)

    scale = 2.0 * eta_step / clusters
    for i in range(group):
        n = (step * group + i) * far_slots
        picked = [blocks_ref[where_ref[n + s]] for s in range(far_slots)]
        tiles = jnp.concatenate([tiles_ref[i, s] for s in range(far_slots)], axis=1)
        spread = jnp.dot(tiles, jnp.concatenate(picked, axis=0), preferred_element_type=jnp.float32)
        affinity = jnp.dot(split(spread), graph2_ref[...], preferred_element_type=jnp.float32)
        here = pl.ds(i * tile, tile)
        logits = part_ref[here, :] + scale * affinity
        logits_ref[here, :] = logits
        total[...] += jnp.sum(jnp.exp(logits).reshape(tile // 8, 8, clusters), axis=0)

    @pl.when(step == pl.num_programs(0) - 1)
    def _():
        mass_ref[...] = jnp.sum(total[...], axis=0, keepdims=True) / nodes_total


def last_kernel(logits_ref, newmass_ref, target_ref, out_ref):
    shift = relax_power * (jnp.log(target_ref[...]) - jnp.log(newmass_ref[...]))
    shifted = logits_ref[...] + shift
    out_ref[...] = shifted - jnp.log(jnp.sum(jnp.exp(shifted), axis=1, keepdims=True))


def local(coupling, tile_vals, tile_cols, cluster_graph, cluster_mass):
    shards = lax.axis_size(NODES)
    my_index = lax.axis_index(NODES)
    blocks_dev, slots = tile_cols.shape
    tile = tile_vals.shape[2]
    rows, clusters = coupling.shape
    far_slots = slots - NEAR
    nodes_total = rows * shards
    far_count = blocks_dev * far_slots
    cap = (far_count + shards - 1) // shards
    blocks = coupling.reshape(blocks_dev, tile, clusters)
    f32, bf16, i32 = jnp.float32, jnp.bfloat16, jnp.int32
    group = 4
    steps = blocks_dev // group

    ends = shards - 1
    left = lax.ppermute(blocks, NODES, [(i, i + 1) for i in range(ends)])
    right = lax.ppermute(blocks, NODES, [(i + 1, i) for i in range(ends)])

    asked = pl.pallas_call(
        functools.partial(requests_kernel, cap, nodes_total),
        out_shape=jax.ShapeDtypeStruct((shards, 2 * clusters), f32),
        in_specs=[VMEM, VMEM],
        out_specs=VMEM,
        name="requests",
    )(tile_cols, coupling)
    heard = lax.all_to_all(
        asked.reshape(shards, 1, 2 * clusters), NODES, split_axis=0, concat_axis=0, tiled=True
    ).reshape(shards, 2 * clusters)
    wanted = heard[:, clusters : clusters + cap].astype(i32).reshape(shards * cap)
    found = pl.pallas_call(
        gather_kernel,
        out_shape=jax.ShapeDtypeStruct((shards * cap, tile, clusters), bf16),
        in_specs=[SMEM, VMEM],
        out_specs=ANY,
        scratch_shapes=[pltpu.SemaphoreType.DMA],
        name="gather",
    )(wanted, blocks)
    fetched = lax.all_to_all(
        found.reshape(shards, cap, tile, clusters), NODES, split_axis=0, concat_axis=0, tiled=True
    ).reshape(shards * cap, tile, clusters)

    base = (my_index * blocks_dev - blocks_dev).astype(i32).reshape(1)
    flops = 2 * rows * clusters
    part, graph2, where = pl.pallas_call(
        functools.partial(near_kernel, group, cap),
        grid=(steps,),
        out_shape=(
            jax.ShapeDtypeStruct((rows, clusters), f32),
            jax.ShapeDtypeStruct((2 * clusters, clusters), bf16),
            jax.ShapeDtypeStruct((far_count,), i32),
        ),
        in_specs=[
            SMEM, SMEM, ANY, ANY, ANY,
            pl.BlockSpec((group, NEAR, tile, tile), lambda i: (i, 0, 0, 0)),
            pl.BlockSpec((group * tile, clusters), lambda i: (i, 0)),
            VMEM, VMEM,
        ],
        out_specs=(pl.BlockSpec((group * tile, clusters), lambda i: (i, 0)), VMEM, SMEM),
        scratch_shapes=[
            pltpu.VMEM((3 * blocks_dev, tile, clusters), bf16),
            pltpu.VMEM((8, clusters), f32),
            pltpu.SMEM((shards,), i32),
            pltpu.SemaphoreType.DMA((3,)),
        ],
        cost_estimate=pl.CostEstimate(
            flops=flops * (NEAR * tile + 2 * clusters), bytes_accessed=16 << 20, transcendentals=rows * clusters
        ),
        name="near",
    )(tile_cols.reshape(-1), base, left, blocks, right, tile_vals, coupling, cluster_graph, heard)

    logits, mass_part = pl.pallas_call(
        functools.partial(far_kernel, group, nodes_total),
        grid=(steps,),
        out_shape=(
            jax.ShapeDtypeStruct((rows, clusters), f32),
            jax.ShapeDtypeStruct((1, clusters), f32),
        ),
        in_specs=[
            SMEM, VMEM,
            pl.BlockSpec((group, far_slots, tile, tile), lambda i: (i, NEAR // far_slots, 0, 0)),
            pl.BlockSpec((group * tile, clusters), lambda i: (i, 0)),
            VMEM,
        ],
        out_specs=(pl.BlockSpec((group * tile, clusters), lambda i: (i, 0)), VMEM),
        scratch_shapes=[pltpu.VMEM((8, clusters), f32)],
        cost_estimate=pl.CostEstimate(
            flops=flops * (far_slots * tile + 2 * clusters), bytes_accessed=8 << 20, transcendentals=rows * clusters
        ),
        name="far",
    )(where, fetched, tile_vals, part, graph2)

    newmass = mass_part
    span = 1
    while span < shards:
        newmass = newmass + lax.ppermute(newmass, NODES, [(i, i ^ span) for i in range(shards)])
        span *= 2

    return pl.pallas_call(
        last_kernel,
        grid=(steps,),
        out_shape=jax.ShapeDtypeStruct((rows, clusters), f32),
        in_specs=[pl.BlockSpec((group * tile, clusters), lambda i: (i, 0)), VMEM, VMEM],
        out_specs=pl.BlockSpec((group * tile, clusters), lambda i: (i, 0)),
        name="last",
    )(logits, newmass, cluster_mass.reshape(1, clusters))


def solution(mesh):
    return jax.shard_map(
        local,
        mesh=mesh,
        in_specs=(
            P(("groups", "rows", "sub"), None),
            P(("groups", "rows", "sub"), None, None, None),
            P(("groups", "rows", "sub"), None),
            P("groups", None),
            P("groups"),
        ),
        out_specs=P(("groups", "rows", "sub"), None),
        check_vma=False,
    )
```

time: 168 us -> 127 us (0.76)
  Pallas kernels: 0 us -> 31.3 us
  blocking collectives: 33.3 us -> 10.1 us
  local copies, waits for them, and re-layouts: 27.4 us -> 4.7 us
  other arithmetic: 21.3 us -> 1.19 us
  matrix products: 20.1 us -> 0 us
  waiting for transfers between devices: 51.8 us -> 66.2 us
  starting transfers between devices: 13.2 us -> 11.2 us
    pallas_call x0 -> x5, Pallas kernels: none -> 31.3 us  [the longest x1 11.4 us: local(): pl.pallas_call(functools.partial(near_kernel, group, cap), grid=(steps,),...]
    psum x1 -> x0, blocking collectives: 23.2 us -> none  [local(): colmass, boost_mass = lax.psum((mass_part, boost_part), ('rows', 'sub'))]
    dot_general x7 -> x0, matrix products: 20.1 us -> none  [the longest x4 13.1 us: local(): jnp.einsum('nij,njk->nik', tile_vals[:, slot_id], picked, preferred_eleme...]
    gather x6 -> x0, local copies, waits for them, and re-layouts: 19.3 us -> none  [the longest x4 14.5 us: local(): picked = jnp.take(window, near_index[:, slot_id], axis=0)]
    concatenate x3 -> x0, other arithmetic: 16.4 us -> none  [the longest x1 16.4 us: padded(): jnp.concatenate([lax.ppermute(tail, axis, [(i, (i + 1) % count) for i in...]
    ppermute x2 -> x6, waiting for transfers between devices: 51.8 us -> 66.2 us  [the longest x1 51.3 us: local(): right = lax.ppermute(blocks, NODES, [(i + 1, i) for i in range(ends)])]
    scatter x1 -> x0, local copies, waits for them, and re-layouts: 3.5 us -> none  [local(): jnp.zeros((shards, capacity), jnp.int32).at[far_owner, far_slot]]
    reduce_sum x1 -> x0, local copies, waits for them, and re-layouts: 3.03 us -> none  [local(): jnp.sum(far_terms.reshape(blocks_dev, far_slots, tile_size, clusters), ax...]
  transfers between devices with their start and end apart: 3 -> 7, of which waited for: 1 -> 6; matrix products, arithmetic and copies ran while one was open for 24% -> 1% of each run, Pallas kernels for 0% -> 9%
where the time goes in v1:
time: 127 us; the launch traced here: 125 us
  waiting for transfers between devices  66.2 us (52%)
  Pallas kernels  31.3 us (25%)
  starting transfers between devices  11.2 us (9%)
  blocking collectives  10.1 us (8%)
  local copies, waits for them, and re-layouts  4.7 us (4%)
    ppermute x1, waiting for transfers between devices, local(): right = lax.ppermute(blocks, NODES, [(i + 1, i) for i in range(ends)])  51.3 us
    ppermute x4, waiting for transfers between devices, local(): lax.ppermute(newmass, NODES, [(i, i ^ span) for i in range(shards)])  12.8 us
    pallas_call x1, Pallas kernels, local(): pl.pallas_call(functools.partial(near_kernel, group, cap), grid=(steps,),...  11.4 us
    all_to_all x1, blocking collectives, local(): lax.all_to_all(asked.reshape(shards, 1, 2 * clusters), NODES, split_axis=...  10.1 us
    pallas_call x1, Pallas kernels, local(): pl.pallas_call(functools.partial(far_kernel, group, nodes_total), grid=(s...  8.3 us
    pallas_call x1, Pallas kernels, local(): pl.pallas_call(last_kernel, grid=(steps,), out_shape=jax.ShapeDtypeStruct...  6.15 us
    all_to_all x1, starting transfers between devices, local(): lax.all_to_all(found.reshape(shards, cap, tile, clusters), NODES, split_a...  6.15 us
    ppermute x1, starting transfers between devices, local(): right = lax.ppermute(blocks, NODES, [(i + 1, i) for i in range(ends)])  3.08 us
  transfers between devices with their start and end apart: 7, of which 6 were waited for; matrix products, arithmetic and copies ran while one was open for 1% of the time, Pallas kernels for 9%

profile of v1, /device:TPU:16, one launch (start us, length us, event | category | flops | bytes accessed | tf_op | source)
XLA Modules:
  0.0 124.7 jit_solution(9550613385754060782)
XLA Ops:
  0.0 1.4 %copy.9.cols_ref = s32[32,6]{1,0:T(8,128)} copy(s32[32,6]{0,1:T(8,128)} %param.7) | data formatting | bytes 1536 | tf_op args[2]
  1.4 2.9 %requests.1 = f32[16,256]{1,0:T(8,128)} custom-call(s32[32,6]{1,0:T(8,128)} %copy.9.cols_ref, bf16[4096,128]{1,0:T(8,128)(2,1)} %rows_ref.1), custom_call_target="tpu_custom_call" | custom-call | tf_op jit(solution)/shard_map/requests/pallas_call | solution.py:193
  4.2 0.7 copy.11
  5.0 10.1 %all_to_all.10 = f32[16,1,256]{2,1,0:T(1,128)S(1)} all-to-all(f32[16,1,256]{2,1,0:T(1,128)S(1)} %copy.11), channel_id=1, replica_groups=mesh['groups'=2,'rows'=8,'sub'=2] {'rows','sub'}, dimensions={0} | all-to-all | bytes 32768 | tf_op jit(solution)/shard_map/all_to_all | solution.py:200
  15.1 0.0 copy-start.3
  15.1 0.6 reshape.32.wanted_ref
  15.7 2.6 %gather.1 = bf16[64,128,128]{2,1,0:T(8,128)(2,1)} custom-call(s32[64]{0:T(128)} %reshape.32.wanted_ref, bf16[32,128,128]{2,1,0:T(8,128)(2,1)} %bitcast.9), custom_call_target="tpu_custom_call" | custom-call | tf_op jit(solution)/shard_map/gather/pallas_call | solution.py:204
  18.3 0.0 copy-start
  18.3 0.0 copy-start.2
  18.3 0.0 copy-done.3
  18.3 6.1 %all-to-all-start.1 = ((bf16[16,4,128,128]{3,2,1,0:T(8,128)(2,1)}), bf16[16,4,128,128]{3,2,1,0:T(8,128)(2,1)S(1)}, u32[]{:S(2)}, u32[]{:S(2)}) async-start(bf16[16,4,128,128]{3,2,1,0:T(8,128)(2,1)} %bitcast.13), calls=%async_computation.1 | async-start | bytes 4194304 | tf_op jit(solution)/shard_map/all_to_all | solution.py:212
  24.5 0.0 copy-done
  24.5 3.1 %collective-permute-start.1 = (bf16[32,128,128]{2,1,0:T(8,128)(2,1)S(1)}, bf16[32,128,128]{2,1,0:T(8,128)(2,1)}, u32[]{:S(2)}, u32[]{:S(2)}) collective-permute-start(bf16[32,128,128]{2,1,0:T(8,128)(2,1)S(1)} %bitcast.11), channel_id=1, source_target_pairs={{1,0},{2,1},{3,2},{4,3},{5,4},{6,5},{7,6},{8,7},{9,8},{10,9},{11,1... | collective-permute-start | bytes 3145736 | tf_op jit(solution)/shard_map/ppermute | solution.py:191
  27.6 1.9 %collective-permute-start = (bf16[32,128,128]{2,1,0:T(8,128)(2,1)S(1)}, bf16[32,128,128]{2,1,0:T(8,128)(2,1)}, u32[]{:S(2)}, u32[]{:S(2)}) collective-permute-start(bf16[32,128,128]{2,1,0:T(8,128)(2,1)S(1)} %bitcast.12), channel_id=1, source_target_pairs={{0,1},{1,2},{2,3},{3,4},{4,5},{5,6},{6,7},{7,8},{8,9},{9,10},{10,1... | collective-permute-start | bytes 3145736 | tf_op jit(solution)/shard_map/ppermute | solution.py:190
  29.5 0.0 copy-done.2
  29.5 0.6 reshape.27.cols_ref
  30.2 51.3 %collective-permute-done.1.right_ref = bf16[32,128,128]{2,1,0:T(8,128)(2,1)} collective-permute-done((bf16[32,128,128]{2,1,0:T(8,128)(2,1)S(1)}, bf16[32,128,128]{2,1,0:T(8,128)(2,1)}, u32[]{:S(2)}, u32[]{:S(2)}) %collective-permute-start.1) | collective-permute-done | bytes 1048608 | tf_op jit(solution)/shard_map/ppermute | solution.py:191
  81.5 2.0 %collective-permute-done.left_ref = bf16[32,128,128]{2,1,0:T(8,128)(2,1)} collective-permute-done((bf16[32,128,128]{2,1,0:T(8,128)(2,1)S(1)}, bf16[32,128,128]{2,1,0:T(8,128)(2,1)}, u32[]{:S(2)}, u32[]{:S(2)}) %collective-permute-start) | collective-permute-done | bytes 1048608 | tf_op jit(solution)/shard_map/ppermute | solution.py:190
  83.5 11.4 %near.1 = (f32[4096,128]{1,0:T(8,128)}, bf16[256,128]{1,0:T(8,128)(2,1)}, s32[64]{0:T(128)}) custom-call(s32[192]{0:T(256)} %reshape.27.cols_ref, s32[1]{0:T(128)} %bitcast.base_ref, bf16[32,128,128]{2,1,0:T(8,128)(2,1)} %collective-permute-done.left_ref, bf16[32,128,128]{2,1,0:T(8,128)(2,1)} %bitcast.10, ...), custom_call_target="tpu_custom_call" | custom-call | flops 805306368 | bytes 16777216 | tf_op jit(solution)/shard_map/near/pallas_call | solution.py:218
  94.9 0.0 all-to-all-done.1
  94.9 0.0 copy-start.1
  94.9 1.3 %copy-done.1 = bf16[16,4,128,128]{3,2,1,0:T(8,128)(2,1)} copy-done((bf16[16,4,128,128]{3,2,1,0:T(8,128)(2,1)}, bf16[16,4,128,128]{3,2,1,0:T(8,128)(2,1)S(1)}, u32[]{:S(2)}) %copy-start.1) | copy-done | bytes 2097176
  96.2 8.3 %far.1 = (f32[4096,128]{1,0:T(8,128)}, f32[1,128]{1,0:T(1,128)}) custom-call(s32[64]{0:T(128)} %get-tuple-element.10.where_ref, bf16[64,128,128]{2,1,0:T(8,128)(2,1)} %bitcast.14, bf16[32,6,128,128]{3,2,1,0:T(8,128)(2,1)} %tiles_ref.3, f32[4096,128]{1,0:T(8,128)} %get-tuple-element.11.part_ref, bf16[256,128]{1,0:T(8,128)(2,1)} %get-tuple-element.12.graph2_ref), custom_call_target="tpu_custom_call" | custom-call | flops 536870912 | bytes 8388608 | tf_op jit(solution)/shard_map/far/pallas_call | solution.py:245
  104.5 0.0 collective-permute-start.2
  104.5 1.2 collective-permute-done.2
  105.8 0.6 add.17
  106.4 0.0 collective-permute-start.3
  106.4 3.6 %collective-permute-done.3 = f32[1,128]{1,0:T(1,128)S(1)} collective-permute-done((f32[1,128]{1,0:T(1,128)S(1)}, f32[1,128]{1,0:T(1,128)S(1)}, u32[]{:S(2)}, u32[]{:S(2)}) %collective-permute-start.3) | collective-permute-done | bytes 544 | tf_op jit(solution)/shard_map/ppermute | solution.py:269
  110.0 0.0 collective-permute-start.4
  110.0 3.6 %collective-permute-done.4 = f32[1,128]{1,0:T(1,128)S(1)} collective-permute-done((f32[1,128]{1,0:T(1,128)S(1)}, f32[1,128]{1,0:T(1,128)S(1)}, u32[]{:S(2)}, u32[]{:S(2)}) %collective-permute-start.4) | collective-permute-done | bytes 544 | tf_op jit(solution)/shard_map/ppermute | solution.py:269
  113.5 0.0 collective-permute-start.5
  113.5 4.5 %collective-permute-done.5 = f32[1,128]{1,0:T(1,128)S(1)} collective-permute-done((f32[1,128]{1,0:T(1,128)S(1)}, f32[1,128]{1,0:T(1,128)S(1)}, u32[]{:S(2)}, u32[]{:S(2)}) %collective-permute-start.5) | collective-permute-done | bytes 544 | tf_op jit(solution)/shard_map/ppermute | solution.py:269
  118.0 0.5 add.20.newmass_ref
  118.5 6.2 %last.1 = f32[4096,128]{1,0:T(8,128)} custom-call(f32[4096,128]{1,0:T(8,128)} %get-tuple-element.13.logits_ref, f32[1,128]{1,0:T(1,128)} %add.20.newmass_ref, f32[1,128]{1,0:T(1,128)} %bitcast.18), custom_call_target="tpu_custom_call" | custom-call | tf_op jit(solution)/shard_map/last/pallas_call | solution.py:272
  (4 shorter events, 0.0 us)
Async XLA Ops:
  15.1 3.2 %copy-start.3 = (f32[16,1,256]{2,0,1:T(8,128)}, f32[16,1,256]{2,0,1:T(8,128)S(1)}, u32[]{:S(2)}) copy-start(f32[16,1,256]{2,0,1:T(8,128)S(1)} %copy.14) | copy-start | bytes 49156
  18.3 6.2 %copy-start = (bf16[4096,128]{1,0:T(8,128)(2,1)S(1)}, bf16[4096,128]{1,0:T(8,128)(2,1)}, u32[]{:S(2)}) copy-start(bf16[4096,128]{1,0:T(8,128)(2,1)} %rows_ref.1) | copy-start | bytes 3145732
  18.3 11.2 %copy-start.2 = (s32[32,6]{1,0:T(8,128)S(1)}, s32[32,6]{1,0:T(8,128)}, u32[]{:S(2)}) copy-start(s32[32,6]{1,0:T(8,128)} %copy.9.cols_ref) | copy-start | bytes 2308
  18.3 76.6 %all-to-all-start.1 = ((bf16[16,4,128,128]{3,2,1,0:T(8,128)(2,1)}), bf16[16,4,128,128]{3,2,1,0:T(8,128)(2,1)S(1)}, u32[]{:S(2)}, u32[]{:S(2)}) async-start(bf16[16,4,128,128]{3,2,1,0:T(8,128)(2,1)} %bitcast.13), calls=%async_computation.1 | async-start | bytes 4194304 | tf_op jit(solution)/shard_map/all_to_all | solution.py:212
  24.5 57.0 %collective-permute-start.1 = (bf16[32,128,128]{2,1,0:T(8,128)(2,1)S(1)}, bf16[32,128,128]{2,1,0:T(8,128)(2,1)}, u32[]{:S(2)}, u32[]{:S(2)}) collective-permute-start(bf16[32,128,128]{2,1,0:T(8,128)(2,1)S(1)} %bitcast.11), channel_id=1, source_target_pairs={{1,0},{2,1},{3,2},{4,3},{5,4},{6,5},{7,6},{8,7},{9,8},{10,9},{11,1... | collective-permute-start | bytes 3145736 | tf_op jit(solution)/shard_map/ppermute | solution.py:191
  27.6 55.9 %collective-permute-start = (bf16[32,128,128]{2,1,0:T(8,128)(2,1)S(1)}, bf16[32,128,128]{2,1,0:T(8,128)(2,1)}, u32[]{:S(2)}, u32[]{:S(2)}) collective-permute-start(bf16[32,128,128]{2,1,0:T(8,128)(2,1)S(1)} %bitcast.12), channel_id=1, source_target_pairs={{0,1},{1,2},{2,3},{3,4},{4,5},{5,6},{6,7},{7,8},{8,9},{9,10},{10,1... | collective-permute-start | bytes 3145736 | tf_op jit(solution)/shard_map/ppermute | solution.py:190
  94.9 1.3 %copy-start.1 = (bf16[16,4,128,128]{3,2,1,0:T(8,128)(2,1)}, bf16[16,4,128,128]{3,2,1,0:T(8,128)(2,1)S(1)}, u32[]{:S(2)}) copy-start(bf16[16,4,128,128]{3,2,1,0:T(8,128)(2,1)S(1)} %all-to-all-done.1) | copy-start | bytes 6291460
  104.5 1.2 collective-permute-start.2
  106.4 3.6 %collective-permute-start.3 = (f32[1,128]{1,0:T(1,128)S(1)}, f32[1,128]{1,0:T(1,128)S(1)}, u32[]{:S(2)}, u32[]{:S(2)}) collective-permute-start(f32[1,128]{1,0:T(1,128)S(1)} %add.17), channel_id=1, source_target_pairs={{0,2},{1,3},{2,0},{3,1},{4,6},{5,7},{6,4},{7,5},{8,10},{9,11},{10,... | collective-permute-start | bytes 1544 | tf_op jit(solution)/shard_map/ppermute | solution.py:269
  110.0 3.6 %collective-permute-start.4 = (f32[1,128]{1,0:T(1,128)S(1)}, f32[1,128]{1,0:T(1,128)S(1)}, u32[]{:S(2)}, u32[]{:S(2)}) collective-permute-start(f32[1,128]{1,0:T(1,128)S(1)} %add.18), channel_id=1, source_target_pairs={{0,4},{1,5},{2,6},{3,7},{4,0},{5,1},{6,2},{7,3},{8,12},{9,13},{10,... | collective-permute-start | bytes 1544 | tf_op jit(solution)/shard_map/ppermute | solution.py:269
  113.5 4.5 %collective-permute-start.5 = (f32[1,128]{1,0:T(1,128)S(1)}, f32[1,128]{1,0:T(1,128)S(1)}, u32[]{:S(2)}, u32[]{:S(2)}) collective-permute-start(f32[1,128]{1,0:T(1,128)S(1)} %add.19), channel_id=1, source_target_pairs={{0,8},{1,9},{2,10},{3,11},{4,12},{5,13},{6,14},{7,15},{8,0},{9,1},... | collective-permute-start | bytes 1544 | tf_op jit(solution)/shard_map/ppermute | solution.py:269
